TPU v7x, 128 devices: a whole 4x4x4 slice. The times are simulated.
128 devices in a mesh: lat: 8 (over y_hi, z), lon: 16 (over x, y_lo, core).
Axes of the slice: x: 4, y: 4 (y_hi: 2, y_lo: 2; y = y_hi * 2 + y_lo), z: 4, core: 2. Of those that a mesh axis runs over, the one named last changes fastest.
Arguments:
- fields: bfloat16 [2, 256, 768, 256], P(None, 'lat', 'lon'), may hold values from -6 to 6
- kernel: bfloat16 [9, 256, 256], replicated, may hold values from -0.125 to 0.125
- conv_bias: float32 [256], replicated, may hold values from -3 to 3
- cotangent: bfloat16 [2, 128, 384, 256], P(None, 'lat', 'lon'), may hold values from -6 to 6
Outputs:
- pooled: bfloat16 [2, 128, 384, 256], P(None, 'lat', 'lon')
- grad_input: bfloat16 [2, 256, 768, 256], P(None, 'lat', 'lon')
- grad_kernel: float32 [9, 256, 256], replicated
- grad_bias: float32 [256], replicated
All inputs are finite; a program needn't handle non-finite values.
Results may differ from a plain program's by a relative error of at most 0.013.
Values may be sent and summed in bfloat16 or wider, within the bound.
No kernel may reach another device: no remote copies, remote signals or barrier semaphores. Data moves between devices by JAX's collectives and lax.ppermute only.
A program may use at most 64 MiB of HBM per device.

v0:
```python
import math
import jax
import jax.numpy as jnp
from jax import lax
from jax.sharding import PartitionSpec as P


def shifted(shard, axis, by):
    size = lax.axis_size(axis)
    return lax.ppermute(shard, axis, [(i, (i + by) % size) for i in range(size)])


def with_halo(shard, sides, width, wrap):
    for axis, dim in sides:
        size, length = (lax.axis_size(axis), shard.shape[dim])
        up = [(i, (i + 1) % size) for i in range(size if wrap else size - 1)]
        down = [(j, i) for i, j in up]
        last = lax.slice_in_dim(shard, length - width, length, axis=dim)
        first = lax.slice_in_dim(shard, 0, width, axis=dim)
        before = lax.ppermute(last, axis, up)
        after = lax.ppermute(first, axis, down)
        shard = jnp.concatenate([before, shard, after], axis=dim)
    return shard


def lat_cosine(rows, first, total):
    index_rows = (first + jnp.arange(rows)).astype(jnp.float32)
    return jnp.cos((index_rows + 0.5) * (math.pi / total) - math.pi / 2)


def extend(field):
    lat_count = lax.axis_size("lat")
    lat_place = lax.axis_index("lat")
    lon_count = lax.axis_size("lon")
    north_row = field[:, :1]
    south_row = field[:, -1:]
    mirror_north, mirror_south = shifted((north_row, south_row), "lon", lon_count // 2)
    rim_rows = with_halo(field, (("lat", 1),), 1, False)
    upper_pad = jnp.where(lat_place == 0, mirror_north, rim_rows[:, :1])
    bottom = jnp.where(lat_place == lat_count - 1, mirror_south, rim_rows[:, -1:])
    tall = jnp.concatenate([upper_pad, field, bottom], axis=1)
    return with_halo(tall, (("lon", 2),), 1, True)


def forward_conv(padded, kernel, rows, cols):
    chans = padded.shape[-1]
    total = jnp.zeros((padded.shape[0] * rows * cols, kernel.shape[2]), jnp.float32)
    for row_off in range(3):
        for col_off in range(3):
            window = padded[:, row_off : row_off + rows, col_off : col_off + cols, :].reshape(
                -1, chans
            )
            total = total + jnp.dot(
                window, kernel[3 * row_off + col_off], preferred_element_type=jnp.float32
            )
    return total.reshape(padded.shape[0], rows, cols, kernel.shape[2])


def back_conv(padded, kernel, rows, cols):
    chans = padded.shape[-1]
    total = jnp.zeros((padded.shape[0] * rows * cols, kernel.shape[1]), jnp.float32)
    for row_off in range(3):
        for col_off in range(3):
            window = padded[
                :, 2 - row_off : 2 - row_off + rows, 2 - col_off : 2 - col_off + cols, :
            ].reshape(-1, chans)
            total = total + lax.dot_general(
                window,
                kernel[3 * row_off + col_off],
                (((1,), (1,)), ((), ())),
                preferred_element_type=jnp.float32,
            )
    return total.reshape(padded.shape[0], rows, cols, kernel.shape[1])


def pole_term(pad_row, kernel, row_off, cols):
    chans = pad_row.shape[-1]
    total = jnp.zeros((pad_row.shape[0] * cols, kernel.shape[1]), jnp.float32)
    for col_off in range(3):
        window = pad_row[:, :, 2 - col_off : 2 - col_off + cols, :].reshape(-1, chans)
        total = total + lax.dot_general(
            window,
            kernel[3 * row_off + col_off],
            (((1,), (1,)), ((), ())),
            preferred_element_type=jnp.float32,
        )
    return total.reshape(pad_row.shape[0], 1, cols, kernel.shape[1])


def kernel_grad(padded, grad_pre, rows, cols):
    chans = padded.shape[-1]
    flat_grad = grad_pre.reshape(-1, grad_pre.shape[-1])
    pieces = []
    for row_off in range(3):
        for col_off in range(3):
            window = padded[:, row_off : row_off + rows, col_off : col_off + cols, :].reshape(
                -1, chans
            )
            pieces.append(
                lax.dot_general(
                    window, flat_grad, (((0,), (0,)), ((), ())), preferred_element_type=jnp.float32
                )
            )
    return jnp.stack(pieces, axis=0)


def local(fields, kernel, conv_bias, cotangent):
    batches, rows, cols, chans = fields.shape
    lat_count = lax.axis_size("lat")
    lat_place = lax.axis_index("lat")
    padded = extend(fields)
    pre = forward_conv(padded, kernel, rows, cols) + conv_bias
    sigma = jax.nn.sigmoid(pre)
    active = (pre * sigma).astype(jnp.bfloat16)
    cosine = lat_cosine(rows, lat_place * rows, rows * lat_count)
    pair_sum = cosine[0::2] + cosine[1::2]
    weighted = active.astype(jnp.float32) * cosine[None, :, None, None]
    pooled = (
        weighted.reshape(batches, rows // 2, 2, cols // 2, 2, chans).sum(axis=(2, 4))
        / (2.0 * pair_sum)[None, :, None, None]
    )
    share = cosine / (2.0 * jnp.repeat(pair_sum, 2))
    spread = jnp.repeat(jnp.repeat(cotangent.astype(jnp.float32), 2, axis=1), 2, axis=2)
    grad_pre = (spread * share[None, :, None, None] * sigma * (1.0 + pre * (1.0 - sigma))).astype(
        jnp.bfloat16
    )
    kernel_part = kernel_grad(padded, grad_pre, rows, cols)
    bias_part = jnp.sum(grad_pre.astype(jnp.float32), axis=(0, 1, 2))
    grad_kernel, grad_bias = lax.psum((kernel_part, bias_part), ("lat", "lon"))
    grad_padded = extend(grad_pre)
    is_north = lat_place == 0
    is_south = lat_place == lat_count - 1
    blank = jnp.zeros_like(grad_padded[:, :1])
    upper_rows = jnp.where(is_north, blank, grad_padded[:, :1])
    lower_rows = jnp.where(is_south, blank, grad_padded[:, -1:])
    inner = jnp.concatenate([upper_rows, grad_padded[:, 1:-1], lower_rows], axis=1)
    back = back_conv(inner, kernel, rows, cols)
    north_add = jnp.where(is_north, pole_term(grad_padded[:, :1], kernel, 0, cols), 0.0)
    south_add = jnp.where(is_south, pole_term(grad_padded[:, -1:], kernel, 2, cols), 0.0)
    back = jnp.concatenate(
        [back[:, :1] + north_add, back[:, 1:-1], back[:, -1:] + south_add], axis=1
    )
    return (pooled.astype(jnp.bfloat16), back.astype(jnp.bfloat16), grad_kernel, grad_bias)


def solution(mesh):
    return jax.shard_map(
        local,
        mesh=mesh,
        in_specs=(P(None, "lat", "lon", None), P(), P(), P(None, "lat", "lon", None)),
        out_specs=(P(None, "lat", "lon", None), P(None, "lat", "lon", None), P(), P()),
        check_vma=False,
    )
```

profile of v0, /device:TPU:1, one launch (start us, length us, event | category | flops | bytes accessed | tf_op | source)
XLA Modules:
  0.0 244.1 jit_solution(9984950914171488139)
XLA Ops:
  7.2 0.8 fusion.107
  8.0 3.6 %collective-permute-start.2 = (bf16[2,1,48,256]{3,2,1,0:T(8,128)(2,1)S(1)}, bf16[2,1,48,256]{3,2,1,0:T(8,128)(2,1)S(1)}, u32[]{:S(2)}, u32[]{:S(2)}) collective-permute-start(bf16[2,1,48,256]{3,2,1,0:T(8,128)(2,1)S(1)} %get-tuple-element.41), channel_id=1, source_target_pairs={{0,8},{1,9},{2,10},{3,11},{4,12},{5,13},{6,14},{7,15},{8,0},{9,1},... | collective-permute-start | bytes 147464 | tf_op jit(solution)/shard_map/ppermute | solution.py:10
  11.7 3.5 %collective-permute-start.1 = (bf16[2,1,48,256]{3,2,1,0:T(8,128)(2,1)S(1)}, bf16[2,1,48,256]{3,2,1,0:T(8,128)(2,1)S(1)}, u32[]{:S(2)}, u32[]{:S(2)}) collective-permute-start(bf16[2,1,48,256]{3,2,1,0:T(8,128)(2,1)S(1)} %get-tuple-element.41), channel_id=1, source_target_pairs={{0,16},{16,32},{32,48},{48,64},{64,80},{80,96},{96,112},{1,17},{17... | collective-permute-start | bytes 147464 | tf_op jit(solution)/shard_map/ppermute | solution.py:20
  15.2 1.3 collective-permute-start.3
  17.4 1.1 broadcast_in_dim.21
  18.5 1.7 broadcast_in_dim.22
  20.3 3.4 %reshape.184 = f32[3072,256]{1,0:T(8,128)} reshape(f32[2,32,24,2,256]{4,3,2,1,0:T(2,128)S(1)} %broadcast_in_dim.22) | data formatting | bytes 6291456 | tf_op jit(solution)/shard_map/reshape | solution.py:123
  23.7 3.4 %reshape.178 = f32[2,32,48,256]{3,2,1,0:T(8,128)} reshape(f32[2,32,24,2,256]{4,3,2,1,0:T(2,128)S(1)} %broadcast_in_dim.22) | data formatting | bytes 6291456 | tf_op jit(solution)/shard_map/reshape | solution.py:123
  27.8 0.7 copy-done
  28.8 1.6 collective-permute-start.5
  30.4 1.4 collective-permute-start.4
  32.4 1.2 collective-permute-done.5
  33.7 1.2 pad_maximum_fusion
  34.9 3.1 %fusion.104 = (bf16[2,32,48,256]{3,2,1,0:T(8,128)(2,1)S(1)}, bf16[2,32,48,256]{3,2,1,0:T(8,128)(2,1)S(1)}, bf16[2,32,48,256]{3,2,1,0:T(8,128)(2,1)S(1)}, bf16[2,...) fusion(bf16[2,34,49,256]{3,2,1,0:T(8,128)(2,1)S(1)} %get-tuple-element., ...), kind=kLoop, calls=%fused_computation.171 | loop fusion | bytes 18874368 | tf_op jit(solution)/shard_map/slice | solution.py:50
  42.1 1.3 copy-done.10
  43.4 2.2 convert_reduce_fusion
  45.6 1.4 multiply_convert_fusion.2
  48.0 1.3 collective-permute-start.9
  49.2 2.8 %collective-permute-start.6 = (bf16[2,1,48,256]{3,2,1,0:T(8,128)(2,1)}, bf16[2,1,48,256]{3,2,1,0:T(8,128)(2,1)}, u32[]{:S(2)}, u32[]{:S(2)}) collective-permute-start(bf16[2,1,48,256]{3,2,1,0:T(8,128)(2,1)} %get-tuple-element.37), channel_id=1, source_target_pairs={{0,8},{1,9},{2,10},{3,11},{4,12},{5,13},{6,14},{7,15},{8,0},{9,1},... | collective-permute-start | bytes 147464 | tf_op jit(solution)/shard_map/ppermute | solution.py:10
  52.3 5.4 %collective-permute-start.7 = (bf16[2,1,48,256]{3,2,1,0:T(8,128)(2,1)}, bf16[2,1,48,256]{3,2,1,0:T(8,128)(2,1)}, u32[]{:S(2)}, u32[]{:S(2)}) collective-permute-start(bf16[2,1,48,256]{3,2,1,0:T(8,128)(2,1)} %get-tuple-element.38), channel_id=1, source_target_pairs={{0,16},{16,32},{32,48},{48,64},{64,80},{80,96},{96,112},{1,17},{17... | collective-permute-start | bytes 147464 | tf_op jit(solution)/shard_map/ppermute | solution.py:20
  57.7 1.3 fusion.21
  59.0 5.2 %reshape.176 = f32[2,16,2,24,2,256]{5,4,3,2,1,0:T(2,128)} reshape(f32[3072,256]{1,0:T(8,128)} %copy-done.4) | data formatting | bytes 6291456 | tf_op jit(solution)/shard_map/reshape | solution.py:56
  64.2 2.8 %fusion.31 = f32[9,256,256]{2,1,0:T(8,128)} fusion(f32[9,256,256]{2,1,0:T(8,128)} %fusion.21, bf16[2,32,48,256]{3,2,1,0:T(8,128)(2,1)S(1)} %multiply_convert_fusion.2, bf16[2,32,48,256]{3,2,1,0:T(8,128)(2,1)} %param.4, bf16[2,1,48,256]{3,2,1,0:T(8,128)(2,1)} %copy-done.14), kind=kOutput, calls=%fused_computation.76 | convolution fusion | flops 405897216 | bytes 3457024 | tf_op jit(solution)/shard_map/dot_general | solution.py:100
  67.1 1.3 fusion.20
  68.4 1.3 fusion.19
  69.8 1.4 fusion.18
  71.3 1.3 fusion.17
  72.6 1.3 fusion.16
  73.9 1.3 fusion.25
  75.2 1.3 fusion.15
  77.3 3.2 %multiply_reduce_fusion = f32[2,16,24,256]{3,2,1,0:T(8,128)S(1)} fusion(f32[16,2]{1,0:T(8,128)S(1)} %add_cosine_fusion, f32[256]{0:T(256)S(1)} %copy-done.18, f32[2,16,2,24,2,256]{5,4,3,2,1,0:T(2,128)} %reshape.176), kind=kLoop, calls=%fused_computation.23 | loop fusion | flops 6881280 | bytes 3933312 | tf_op jit(solution)/shard_map/reduce_sum | solution.py:119
  80.5 0.9 divide_convert_fusion
  81.4 72.1 %psum.15 = f32[256]{0:T(256)} all-reduce(f32[256]{0:T(256)S(1)} %copy-done.21), channel_id=1, replica_groups=mesh['lat'=8,'lon'=16] {'lat','lon'}, use_global_device_ids=true, to_apply=%region_3.4 | all-reduce | flops 256 | bytes 2048 | tf_op jit(solution)/shard_map/psum | solution.py:129
  153.5 0.8 broadcast_select_fusion.2
  154.5 0.8 broadcast_select_fusion
  155.4 0.9 collective-permute-start.11
  156.3 1.6 collective-permute-start.10
  158.1 1.5 collective-permute-done.11
  159.6 1.1 pad_maximum_fusion.1
  160.8 1.2 maximum_maximum_fusion.1
  162.2 0.8 slice.258
  163.7 2.1 pad_maximum_fusion.3
  168.3 1.3 copy-done.5
  169.5 1.0 copy-done.11
  170.5 1.5 convolution_add_fusion.4
  175.5 1.3 pad_maximum_fusion.7
  176.8 57.3 %all-reduce.2.cloned.1.call-done = f32[9,256,256]{2,1,0:T(8,128)} async-done(((f32[9,256,256]{2,1,0:T(8,128)}), f32[9,256,256]{2,1,0:T(8,128)}) %all-reduce.2.cloned.1.call-update) | async-done | bytes 2359312 | tf_op jit(solution)/shard_map/psum | solution.py:129
  234.1 3.2 %copy.45 = f32[9,256,256]{2,1,0:T(8,128)} copy(f32[9,256,256]{2,1,0:T(8,128)} %all-reduce.2.cloned.1.call-done) | data formatting | bytes 4718592
  (101 shorter events, 15.8 us)
Async XLA Ops:
  7.2 226.9 %all-reduce.2.cloned.1.call-start = ((), (), s32[]{:S(2)}) async-start(), calls=%async_computation | async-start | bytes 4718592 | tf_op jit(solution)/shard_map/psum | solution.py:129
  8.0 19.7 %collective-permute-start.2 = (bf16[2,1,48,256]{3,2,1,0:T(8,128)(2,1)S(1)}, bf16[2,1,48,256]{3,2,1,0:T(8,128)(2,1)S(1)}, u32[]{:S(2)}, u32[]{:S(2)}) collective-permute-start(bf16[2,1,48,256]{3,2,1,0:T(8,128)(2,1)S(1)} %get-tuple-element.41), channel_id=1, source_target_pairs={{0,8},{1,9},{2,10},{3,11},{4,12},{5,13},{6,14},{7,15},{8,0},{9,1},... | collective-permute-start | bytes 147464 | tf_op jit(solution)/shard_map/ppermute | solution.py:10
  11.7 16.1 %collective-permute-start.1 = (bf16[2,1,48,256]{3,2,1,0:T(8,128)(2,1)S(1)}, bf16[2,1,48,256]{3,2,1,0:T(8,128)(2,1)S(1)}, u32[]{:S(2)}, u32[]{:S(2)}) collective-permute-start(bf16[2,1,48,256]{3,2,1,0:T(8,128)(2,1)S(1)} %get-tuple-element.41), channel_id=1, source_target_pairs={{0,16},{16,32},{32,48},{48,64},{64,80},{80,96},{96,112},{1,17},{17... | collective-permute-start | bytes 147464 | tf_op jit(solution)/shard_map/ppermute | solution.py:20
  15.2 12.5 %collective-permute-start.3 = (bf16[2,1,48,256]{3,2,1,0:T(8,128)(2,1)S(1)}, bf16[2,1,48,256]{3,2,1,0:T(8,128)(2,1)S(1)}, u32[]{:S(2)}, u32[]{:S(2)}) collective-permute-start(bf16[2,1,48,256]{3,2,1,0:T(8,128)(2,1)S(1)} %get-tuple-element.42), channel_id=1, source_target_pairs={{16,0},{32,16},{48,32},{64,48},{80,64},{96,80},{112,96},{17,1},{33... | collective-permute-start | bytes 147464 | tf_op jit(solution)/shard_map/ppermute | solution.py:21
  16.5 11.3 %collective-permute-start = (bf16[2,1,48,256]{3,2,1,0:T(8,128)(2,1)S(1)}, bf16[2,1,48,256]{3,2,1,0:T(8,128)(2,1)S(1)}, u32[]{:S(2)}, u32[]{:S(2)}) collective-permute-start(bf16[2,1,48,256]{3,2,1,0:T(8,128)(2,1)S(1)} %get-tuple-element.42), channel_id=1, source_target_pairs={{0,8},{1,9},{2,10},{3,11},{4,12},{5,13},{6,14},{7,15},{8,0},{9,1},... | collective-permute-start | bytes 147464 | tf_op jit(solution)/shard_map/ppermute | solution.py:10
  17.1 1.4 copy-start.19
  17.3 9.9 %copy-start.15 = (f32[32]{0:T(128)}, f32[32]{0:T(128)S(1)}, u32[]{:S(2)}) copy-start(f32[32]{0:T(128)S(1)} %fusion.97) | copy-start | bytes 388
  27.1 1.4 copy-start
  27.8 5.9 %copy-start.12 = (bf16[2,1,48,256]{3,2,1,0:T(8,128)(2,1)}, bf16[2,1,48,256]{3,2,1,0:T(8,128)(2,1)S(1)}, u32[]{:S(2)}) copy-start(bf16[2,1,48,256]{3,2,1,0:T(8,128)(2,1)S(1)} %broadcast_select_fusion.1) | copy-start | bytes 147460
  28.5 5.2 %copy-start.14 = (bf16[2,1,48,256]{3,2,1,0:T(8,128)(2,1)}, bf16[2,1,48,256]{3,2,1,0:T(8,128)(2,1)S(1)}, u32[]{:S(2)}) copy-start(bf16[2,1,48,256]{3,2,1,0:T(8,128)(2,1)S(1)} %broadcast_select_fusion.3) | copy-start | bytes 147460
  28.6 3.3 %copy-start.8 = (bf16[9,256,256]{2,1,0:T(8,128)(2,1)S(1)}, bf16[9,256,256]{2,1,0:T(8,128)(2,1)}, u32[]{:S(2)}) copy-start(bf16[9,256,256]{2,1,0:T(8,128)(2,1)} %param.5) | copy-start | bytes 3538948
  28.8 4.8 %collective-permute-start.5 = (bf16[2,34,1,256]{3,2,1,0:T(2,128)(2,1)S(1)}, bf16[2,34,1,256]{3,2,1,0:T(2,128)(2,1)S(1)}, u32[]{:S(2)}, u32[]{:S(2)}) collective-permute-start(bf16[2,34,1,256]{3,2,1,0:T(2,128)(2,1)S(1)} %get-tuple-element.35), channel_id=1, source_target_pairs={{1,0},{2,1},{3,2},{4,3},{5,4},{6,5},{7,6},{8,7},{9,8},{10,9},{11,1... | collective-permute-start | bytes 104456 | tf_op jit(solution)/shard_map/ppermute | solution.py:21
  30.4 3.3 %collective-permute-start.4 = (bf16[2,34,1,256]{3,2,1,0:T(2,128)(2,1)S(1)}, bf16[2,34,1,256]{3,2,1,0:T(2,128)(2,1)S(1)}, u32[]{:S(2)}, u32[]{:S(2)}) collective-permute-start(bf16[2,34,1,256]{3,2,1,0:T(2,128)(2,1)S(1)} %get-tuple-element.36), channel_id=1, source_target_pairs={{0,1},{1,2},{2,3},{3,4},{4,5},{5,6},{6,7},{7,8},{8,9},{9,10},{10,1... | collective-permute-start | bytes 104456 | tf_op jit(solution)/shard_map/ppermute | solution.py:20
  34.9 3.1 %copy-start.2 = (bf16[2,34,49,256]{3,2,1,0:T(8,128)(2,1)}, bf16[2,34,49,256]{3,2,1,0:T(8,128)(2,1)S(1)}, u32[]{:S(2)}) copy-start(bf16[2,34,49,256]{3,2,1,0:T(8,128)(2,1)S(1)} %get-tuple-element.33) | copy-start | bytes 5117956
  41.5 1.9 copy-start.10
  41.5 1.9 copy-start.17
  43.4 2.2 copy-start.6
  43.4 2.2 copy-start.16
  45.6 1.7 copy-start.4
  48.0 106.5 %collective-permute-start.9 = (bf16[2,1,48,256]{3,2,1,0:T(8,128)(2,1)}, bf16[2,1,48,256]{3,2,1,0:T(8,128)(2,1)}, u32[]{:S(2)}, u32[]{:S(2)}) collective-permute-start(bf16[2,1,48,256]{3,2,1,0:T(8,128)(2,1)} %get-tuple-element.37), channel_id=1, source_target_pairs={{16,0},{32,16},{48,32},{64,48},{80,64},{96,80},{112,96},{17,1},{33... | collective-permute-start | bytes 147464 | tf_op jit(solution)/shard_map/ppermute | solution.py:21
  49.2 104.2 %collective-permute-start.6 = (bf16[2,1,48,256]{3,2,1,0:T(8,128)(2,1)}, bf16[2,1,48,256]{3,2,1,0:T(8,128)(2,1)}, u32[]{:S(2)}, u32[]{:S(2)}) collective-permute-start(bf16[2,1,48,256]{3,2,1,0:T(8,128)(2,1)} %get-tuple-element.37), channel_id=1, source_target_pairs={{0,8},{1,9},{2,10},{3,11},{4,12},{5,13},{6,14},{7,15},{8,0},{9,1},... | collective-permute-start | bytes 147464 | tf_op jit(solution)/shard_map/ppermute | solution.py:10
  52.1 102.4 %collective-permute-start.8 = (bf16[2,1,48,256]{3,2,1,0:T(8,128)(2,1)}, bf16[2,1,48,256]{3,2,1,0:T(8,128)(2,1)}, u32[]{:S(2)}, u32[]{:S(2)}) collective-permute-start(bf16[2,1,48,256]{3,2,1,0:T(8,128)(2,1)} %get-tuple-element.38), channel_id=1, source_target_pairs={{0,8},{1,9},{2,10},{3,11},{4,12},{5,13},{6,14},{7,15},{8,0},{9,1},... | collective-permute-start | bytes 147464 | tf_op jit(solution)/shard_map/ppermute | solution.py:10
  52.3 101.2 %collective-permute-start.7 = (bf16[2,1,48,256]{3,2,1,0:T(8,128)(2,1)}, bf16[2,1,48,256]{3,2,1,0:T(8,128)(2,1)}, u32[]{:S(2)}, u32[]{:S(2)}) collective-permute-start(bf16[2,1,48,256]{3,2,1,0:T(8,128)(2,1)} %get-tuple-element.38), channel_id=1, source_target_pairs={{0,16},{16,32},{32,48},{48,64},{64,80},{80,96},{96,112},{1,17},{17... | collective-permute-start | bytes 147464 | tf_op jit(solution)/shard_map/ppermute | solution.py:20
  64.2 2.9 %copy-start.3 = (bf16[2,34,49,256]{3,2,1,0:T(8,128)(2,1)S(1)}, bf16[2,34,49,256]{3,2,1,0:T(8,128)(2,1)}, u32[]{:S(2)}) copy-start(bf16[2,34,49,256]{3,2,1,0:T(8,128)(2,1)} %copy-done.2) | copy-start | bytes 5117956
  68.4 1.4 copy-start.1
  72.6 1.3 copy-start.13
  76.6 0.7 copy-start.18
  77.3 3.2 %copy-start.20 = (f32[16]{0:T(128)S(1)}, f32[16]{0:T(128)}, u32[]{:S(2)}) copy-start(f32[16]{0:T(128)} %copy-done.19) | copy-start | bytes 196
  77.3 4.1 %copy-start.21 = (f32[256]{0:T(256)S(1)}, f32[256]{0:T(256)}, u32[]{:S(2)}) copy-start(f32[256]{0:T(256)} %get-tuple-element.43) | copy-start | bytes 3076
  77.3 77.0 %copy-start.9 = (bf16[9,256,256]{2,1,0:T(8,128)(2,1)S(1)}, bf16[9,256,256]{2,1,0:T(8,128)(2,1)}, u32[]{:S(2)}) copy-start(bf16[9,256,256]{2,1,0:T(8,128)(2,1)} %param.5) | copy-start | bytes 3538948
  155.4 4.1 %collective-permute-start.11 = (bf16[2,34,1,256]{3,2,1,0:T(2,128)(2,1)S(1)}, bf16[2,34,1,256]{3,2,1,0:T(2,128)(2,1)S(1)}, u32[]{:S(2)}, u32[]{:S(2)}) collective-permute-start(bf16[2,34,1,256]{3,2,1,0:T(2,128)(2,1)S(1)} %get-tuple-element.31), channel_id=1, source_target_pairs={{1,0},{2,1},{3,2},{4,3},{5,4},{6,5},{7,6},{8,7},{9,8},{10,9},{11,1... | collective-permute-start | bytes 104456 | tf_op jit(solution)/shard_map/ppermute | solution.py:21
  156.3 3.3 %collective-permute-start.10 = (bf16[2,34,1,256]{3,2,1,0:T(2,128)(2,1)S(1)}, bf16[2,34,1,256]{3,2,1,0:T(2,128)(2,1)S(1)}, u32[]{:S(2)}, u32[]{:S(2)}) collective-permute-start(bf16[2,34,1,256]{3,2,1,0:T(2,128)(2,1)S(1)} %get-tuple-element.32), channel_id=1, source_target_pairs={{0,1},{1,2},{2,3},{3,4},{4,5},{5,6},{6,7},{7,8},{8,9},{9,10},{10,1... | collective-permute-start | bytes 104456 | tf_op jit(solution)/shard_map/ppermute | solution.py:20
  160.7 1.3 copy-start.7
  162.2 1.5 slice-start
  167.6 1.9 copy-start.5
  167.6 2.8 %copy-start.11 = (f32[3072,256]{1,0:T(8,128)S(1)}, f32[3072,256]{1,0:T(8,128)}, u32[]{:S(2)}) copy-start(f32[3072,256]{1,0:T(8,128)} %reshape.184) | copy-start | bytes 9437188
Sparse Core Ops, SparseCore 0:
  76.7 157.3 all-reduce.1
where the time goes:
time: 245 us; the launch traced here: 244 us
  blocking collectives  72.1 us (29%)
  waiting for transfers between devices  60.1 us (25%)
  local copies, waits for them, and re-layouts  30.9 us (13%)
  matrix products  27.7 us (11%)
  starting transfers between devices  24.1 us (10%)
  other arithmetic  14.8 us (6%)
  between operations  14.5 us (6%)
    psum x1, blocking collectives, local(): grad_kernel, grad_bias = lax.psum((kernel_part, bias_part), ('lat', 'lon'))  72.1 us
    psum x1, waiting for transfers between devices, local(): grad_kernel, grad_bias = lax.psum((kernel_part, bias_part), ('lat', 'lon'))  57.3 us
    dot_general x9, matrix products, kernel_grad(): lax.dot_general(window, flat_grad, (((0,), (0,)), ((), ())), preferred_el...  13.5 us
    ppermute x4, starting transfers between devices, with_halo(): before = lax.ppermute(last, axis, up)  12 us
    unnamed x45, local copies, waits for them, and re-layouts  8.65 us
    ppermute x4, starting transfers between devices, shifted(): lax.ppermute(shard, axis, [(i, (i + by) % size) for i in range(size)])  6.98 us
    reshape x2, local copies, waits for them, and re-layouts, local(): jnp.repeat(jnp.repeat(cotangent.astype(jnp.float32), 2, axis=1), 2, axis=2)  6.82 us
    dot_general x9, matrix products, forward_conv(): jnp.dot(window, kernel[3 * row_off + col_off], preferred_element_type=jnp...  6.79 us
  transfers between devices with their start and end apart: 13, of which 4 were waited for; matrix products, arithmetic and copies ran while one was open for 21% of the time, Pallas kernels for 0%

commit v1 on v0

--- a/solution.py
+++ b/solution.py
@@ -126,7 +126,7 @@
     )
     kernel_part = kernel_grad(padded, grad_pre, rows, cols)
     bias_part = jnp.sum(grad_pre.astype(jnp.float32), axis=(0, 1, 2))
-    grad_kernel, grad_bias = lax.psum((kernel_part, bias_part), ("lat", "lon"))
+    grad_kernel, grad_bias = lax.psum(lax.psum((kernel_part, bias_part), "lat"), "lon")
     grad_padded = extend(grad_pre)
     is_north = lat_place == 0
     is_south = lat_place == lat_count - 1

time: 245 us -> 312 us (1.27)
  waiting for transfers between devices: 60.1 us -> 136 us
  blocking collectives: 72.1 us -> 56.8 us
  matrix products: 27.7 us -> 31.9 us
    psum x1 -> x2, waiting for transfers between devices: 57.3 us -> 132 us  [the longest x1 123 us: local(): lax.psum(lax.psum((kernel_part, bias_part), 'lat'), 'lon')]
    psum x1 -> x2, blocking collectives: 72.1 us -> 56.8 us  [the longest x1 36.5 us: local(): lax.psum(lax.psum((kernel_part, bias_part), 'lat'), 'lon')]
    dot_general x9, matrix products: 6.33 us -> 10.5 us  [back_conv(): lax.dot_general(window, kernel[3 * row_off + col_off], (((1,), (1,)), (()...]
    unnamed x45 -> x49, local copies, waits for them, and re-layouts: 8.65 us -> 9.38 us
  transfers between devices with their start and end apart: 13 -> 14, of which waited for: 4 -> 5; matrix products, arithmetic and copies ran while one was open for 21% -> 18% of each run, Pallas kernels for 0% -> 0%
where the time goes in v1:
time: 312 us
  waiting for transfers between devices  136 us (44%)
  blocking collectives  56.8 us (18%)
  matrix products  31.9 us (10%)
  local copies, waits for them, and re-layouts  31.6 us (10%)
  starting transfers between devices  23.4 us (8%)
  other arithmetic  17.1 us (5%)
  between operations  14.5 us (5%)
    psum x1, waiting for transfers between devices, local(): lax.psum(lax.psum((kernel_part, bias_part), 'lat'), 'lon')  123 us
    psum x1, blocking collectives, local(): lax.psum(lax.psum((kernel_part, bias_part), 'lat'), 'lon')  36.5 us
    psum x1, blocking collectives, local(): lax.psum((kernel_part, bias_part), 'lat')  20.3 us
    dot_general x9, matrix products, kernel_grad(): lax.dot_general(window, flat_grad, (((0,), (0,)), ((), ())), preferred_el...  13.5 us
    ppermute x4, starting transfers between devices, with_halo(): before = lax.ppermute(last, axis, up)  11.4 us
    dot_general x9, matrix products, back_conv(): lax.dot_general(window, kernel[3 * row_off + col_off], (((1,), (1,)), (()...  10.5 us
    unnamed x49, local copies, waits for them, and re-layouts  9.38 us
    psum x1, waiting for transfers between devices, local(): lax.psum((kernel_part, bias_part), 'lat')  9.15 us
  transfers between devices with their start and end apart: 14, of which 5 were waited for; matrix products, arithmetic and copies ran while one was open for 18% of the time, Pallas kernels for 0%

profile of v1, /device:TPU:1, one launch (start us, length us, event | category | flops | bytes accessed | tf_op | source)
XLA Modules:
  0.0 311.6 jit_solution(14044216192749639522)
XLA Ops:
  7.2 0.8 fusion.107
  8.0 3.6 %collective-permute-start.2 = (bf16[2,1,48,256]{3,2,1,0:T(8,128)(2,1)S(1)}, bf16[2,1,48,256]{3,2,1,0:T(8,128)(2,1)S(1)}, u32[]{:S(2)}, u32[]{:S(2)}) collective-permute-start(bf16[2,1,48,256]{3,2,1,0:T(8,128)(2,1)S(1)} %get-tuple-element.41), channel_id=1, source_target_pairs={{0,8},{1,9},{2,10},{3,11},{4,12},{5,13},{6,14},{7,15},{8,0},{9,1},... | collective-permute-start | bytes 147464 | tf_op jit(solution)/shard_map/ppermute | solution.py:10
  11.7 3.5 %collective-permute-start.1 = (bf16[2,1,48,256]{3,2,1,0:T(8,128)(2,1)S(1)}, bf16[2,1,48,256]{3,2,1,0:T(8,128)(2,1)S(1)}, u32[]{:S(2)}, u32[]{:S(2)}) collective-permute-start(bf16[2,1,48,256]{3,2,1,0:T(8,128)(2,1)S(1)} %get-tuple-element.41), channel_id=1, source_target_pairs={{0,16},{16,32},{32,48},{48,64},{64,80},{80,96},{96,112},{1,17},{17... | collective-permute-start | bytes 147464 | tf_op jit(solution)/shard_map/ppermute | solution.py:20
  15.2 1.3 collective-permute-start.3
  17.4 1.1 broadcast_in_dim.21
  18.5 1.7 broadcast_in_dim.22
  20.3 3.4 %reshape.184 = f32[3072,256]{1,0:T(8,128)} reshape(f32[2,32,24,2,256]{4,3,2,1,0:T(2,128)S(1)} %broadcast_in_dim.22) | data formatting | bytes 6291456 | tf_op jit(solution)/shard_map/reshape | solution.py:123
  23.7 3.4 %reshape.178 = f32[2,32,48,256]{3,2,1,0:T(8,128)} reshape(f32[2,32,24,2,256]{4,3,2,1,0:T(2,128)S(1)} %broadcast_in_dim.22) | data formatting | bytes 6291456 | tf_op jit(solution)/shard_map/reshape | solution.py:123
  28.8 1.6 collective-permute-start.5
  30.4 1.4 collective-permute-start.4
  32.4 1.2 collective-permute-done.5
  33.7 1.2 pad_maximum_fusion
  34.9 3.1 fusion.104
  42.1 1.3 copy-done.12
  43.4 2.2 convert_reduce_fusion
  45.6 1.4 multiply_convert_fusion.2
  48.0 1.3 collective-permute-start.9
  49.2 2.8 collective-permute-start.6
  52.3 5.4 %collective-permute-start.7 = (bf16[2,1,48,256]{3,2,1,0:T(8,128)(2,1)}, bf16[2,1,48,256]{3,2,1,0:T(8,128)(2,1)}, u32[]{:S(2)}, u32[]{:S(2)}) collective-permute-start(bf16[2,1,48,256]{3,2,1,0:T(8,128)(2,1)} %get-tuple-element.38), channel_id=1, source_target_pairs={{0,16},{16,32},{32,48},{48,64},{64,80},{80,96},{96,112},{1,17},{17... | collective-permute-start | bytes 147464 | tf_op jit(solution)/shard_map/ppermute | solution.py:20
  57.7 1.3 fusion.21
  59.0 5.2 %reshape.176 = f32[2,16,2,24,2,256]{5,4,3,2,1,0:T(2,128)} reshape(f32[3072,256]{1,0:T(8,128)} %copy-done.4) | data formatting | bytes 6291456 | tf_op jit(solution)/shard_map/reshape | solution.py:56
  64.2 2.8 fusion.31
  67.1 1.3 fusion.20
  68.4 1.3 fusion.19
  69.8 1.4 fusion.18
  71.3 1.3 fusion.17
  72.6 1.3 fusion.16
  73.9 1.3 fusion.25
  75.3 1.3 fusion.15
  77.3 3.1 %multiply_reduce_fusion = f32[2,16,24,256]{3,2,1,0:T(8,128)S(1)} fusion(f32[16,2]{1,0:T(8,128)S(1)} %add_cosine_fusion, f32[256]{0:T(256)S(1)} %copy-done.20, f32[2,16,2,24,2,256]{5,4,3,2,1,0:T(2,128)} %reshape.176), kind=kLoop, calls=%fused_computation.23 | loop fusion | flops 6881280 | bytes 3933312 | tf_op jit(solution)/shard_map/reduce_sum | solution.py:119
  80.4 0.9 divide_convert_fusion
  81.3 20.3 %psum.30 = f32[256]{0:T(256)S(1)} all-reduce(f32[256]{0:T(256)S(1)} %copy-done.23), channel_id=1, replica_groups=mesh['lat'=8,'lon'=16] {'lat'}, use_global_device_ids=true, to_apply=%region_4.5 | all-reduce | flops 256 | bytes 2048 | tf_op jit(solution)/shard_map/psum | solution.py:129
  101.5 36.5 %psum.31 = f32[256]{0:T(256)} all-reduce(f32[256]{0:T(256)S(1)} %psum.30), channel_id=1, replica_groups=mesh['lat'=8,'lon'=16] {'lon'}, use_global_device_ids=true, to_apply=%region_5.6 | all-reduce | flops 256 | bytes 2048 | tf_op jit(solution)/shard_map/psum | solution.py:129
  140.9 1.0 collective-permute-start.10
  142.0 3.1 %collective-permute-done.11 = bf16[2,34,1,256]{3,2,1,0:T(2,128)(2,1)S(1)} collective-permute-done((bf16[2,34,1,256]{3,2,1,0:T(2,128)(2,1)S(1)}, bf16[2,34,1,256]{3,2,1,0:T(2,128)(2,1)S(1)}, u32[]{:S(2)}, u32[]{:S(2)}) %collective-permute-start.11) | collective-permute-done | bytes 34848 | tf_op jit(solution)/shard_map/ppermute | solution.py:21
  145.1 1.1 pad_maximum_fusion.1
  146.3 1.2 maximum_maximum_fusion.1
  147.8 0.8 slice.258
  149.3 4.5 %pad_maximum_fusion.3 = (bf16[2,32,48,256]{3,2,1,0:T(8,128)(2,1)}, bf16[2,32,48,256]{3,2,1,0:T(8,128)(2,1)}, bf16[2,32,48,256]{3,2,1,0:T(8,128)(2,1)}, bf16[2,32...) fusion(bf16[2,32,50,256]{3,2,1,0:T(8,128)(2,1)S(1)} %slice-done, ...), kind=kLoop, calls=%fused_computation.51 | loop fusion | flops 18874368 | bytes 11177984 | tf_op jit(solution)/shard_map/concatenate | solution.py:136
  156.2 1.3 copy-done.5
  157.5 1.0 copy-done.13
  158.5 1.5 convolution_add_fusion.4
  159.9 2.2 convolution_add_fusion.3
  162.2 9.2 %all-reduce.3.cloned.1.call-done = f32[9,256,256]{2,1,0:T(8,128)} async-done(((f32[9,256,256]{2,1,0:T(8,128)}), f32[9,256,256]{2,1,0:T(8,128)}) %all-reduce.3.cloned.1.call-update) | async-done | bytes 2359312 | tf_op jit(solution)/shard_map/psum | solution.py:129
  171.4 3.1 convolution_add_fusion.2
  177.6 1.3 pad_maximum_fusion.7
  178.9 122.6 %all-reduce.5.cloned.1.call-done = f32[9,256,256]{2,1,0:T(8,128)} async-done(((f32[9,256,256]{2,1,0:T(8,128)}), f32[9,256,256]{2,1,0:T(8,128)}) %all-reduce.5.cloned.1.call-update) | async-done | bytes 2359312 | tf_op jit(solution)/shard_map/psum | solution.py:129
  301.6 3.2 %copy.46 = f32[9,256,256]{2,1,0:T(8,128)} copy(f32[9,256,256]{2,1,0:T(8,128)} %all-reduce.5.cloned.1.call-done) | data formatting | bytes 4718592
  (109 shorter events, 18.5 us)
Async XLA Ops:
  7.2 164.2 %all-reduce.3.cloned.1.call-start = ((), (), s32[]{:S(2)}) async-start(), calls=%async_computation | async-start | bytes 4718592 | tf_op jit(solution)/shard_map/psum | solution.py:129
  8.0 19.7 %collective-permute-start.2 = (bf16[2,1,48,256]{3,2,1,0:T(8,128)(2,1)S(1)}, bf16[2,1,48,256]{3,2,1,0:T(8,128)(2,1)S(1)}, u32[]{:S(2)}, u32[]{:S(2)}) collective-permute-start(bf16[2,1,48,256]{3,2,1,0:T(8,128)(2,1)S(1)} %get-tuple-element.41), channel_id=1, source_target_pairs={{0,8},{1,9},{2,10},{3,11},{4,12},{5,13},{6,14},{7,15},{8,0},{9,1},... | collective-permute-start | bytes 147464 | tf_op jit(solution)/shard_map/ppermute | solution.py:10
  11.7 16.1 %collective-permute-start.1 = (bf16[2,1,48,256]{3,2,1,0:T(8,128)(2,1)S(1)}, bf16[2,1,48,256]{3,2,1,0:T(8,128)(2,1)S(1)}, u32[]{:S(2)}, u32[]{:S(2)}) collective-permute-start(bf16[2,1,48,256]{3,2,1,0:T(8,128)(2,1)S(1)} %get-tuple-element.41), channel_id=1, source_target_pairs={{0,16},{16,32},{32,48},{48,64},{64,80},{80,96},{96,112},{1,17},{17... | collective-permute-start | bytes 147464 | tf_op jit(solution)/shard_map/ppermute | solution.py:20
  15.2 12.5 %collective-permute-start.3 = (bf16[2,1,48,256]{3,2,1,0:T(8,128)(2,1)S(1)}, bf16[2,1,48,256]{3,2,1,0:T(8,128)(2,1)S(1)}, u32[]{:S(2)}, u32[]{:S(2)}) collective-permute-start(bf16[2,1,48,256]{3,2,1,0:T(8,128)(2,1)S(1)} %get-tuple-element.42), channel_id=1, source_target_pairs={{16,0},{32,16},{48,32},{64,48},{80,64},{96,80},{112,96},{17,1},{33... | collective-permute-start | bytes 147464 | tf_op jit(solution)/shard_map/ppermute | solution.py:21
  16.5 11.3 %collective-permute-start = (bf16[2,1,48,256]{3,2,1,0:T(8,128)(2,1)S(1)}, bf16[2,1,48,256]{3,2,1,0:T(8,128)(2,1)S(1)}, u32[]{:S(2)}, u32[]{:S(2)}) collective-permute-start(bf16[2,1,48,256]{3,2,1,0:T(8,128)(2,1)S(1)} %get-tuple-element.42), channel_id=1, source_target_pairs={{0,8},{1,9},{2,10},{3,11},{4,12},{5,13},{6,14},{7,15},{8,0},{9,1},... | collective-permute-start | bytes 147464 | tf_op jit(solution)/shard_map/ppermute | solution.py:10
  17.1 1.4 copy-start.21
  17.3 9.9 %copy-start.17 = (f32[32]{0:T(128)}, f32[32]{0:T(128)S(1)}, u32[]{:S(2)}) copy-start(f32[32]{0:T(128)S(1)} %fusion.97) | copy-start | bytes 388
  27.1 1.4 copy-start
  27.8 5.9 %copy-start.14 = (bf16[2,1,48,256]{3,2,1,0:T(8,128)(2,1)}, bf16[2,1,48,256]{3,2,1,0:T(8,128)(2,1)S(1)}, u32[]{:S(2)}) copy-start(bf16[2,1,48,256]{3,2,1,0:T(8,128)(2,1)S(1)} %broadcast_select_fusion.1) | copy-start | bytes 147460
  28.5 5.2 %copy-start.16 = (bf16[2,1,48,256]{3,2,1,0:T(8,128)(2,1)}, bf16[2,1,48,256]{3,2,1,0:T(8,128)(2,1)S(1)}, u32[]{:S(2)}) copy-start(bf16[2,1,48,256]{3,2,1,0:T(8,128)(2,1)S(1)} %broadcast_select_fusion.3) | copy-start | bytes 147460
  28.6 3.3 %copy-start.8 = (bf16[9,256,256]{2,1,0:T(8,128)(2,1)S(1)}, bf16[9,256,256]{2,1,0:T(8,128)(2,1)}, u32[]{:S(2)}) copy-start(bf16[9,256,256]{2,1,0:T(8,128)(2,1)} %param.5) | copy-start | bytes 3538948
  28.8 4.8 %collective-permute-start.5 = (bf16[2,34,1,256]{3,2,1,0:T(2,128)(2,1)S(1)}, bf16[2,34,1,256]{3,2,1,0:T(2,128)(2,1)S(1)}, u32[]{:S(2)}, u32[]{:S(2)}) collective-permute-start(bf16[2,34,1,256]{3,2,1,0:T(2,128)(2,1)S(1)} %get-tuple-element.35), channel_id=1, source_target_pairs={{1,0},{2,1},{3,2},{4,3},{5,4},{6,5},{7,6},{8,7},{9,8},{10,9},{11,1... | collective-permute-start | bytes 104456 | tf_op jit(solution)/shard_map/ppermute | solution.py:21
  30.4 3.3 %collective-permute-start.4 = (bf16[2,34,1,256]{3,2,1,0:T(2,128)(2,1)S(1)}, bf16[2,34,1,256]{3,2,1,0:T(2,128)(2,1)S(1)}, u32[]{:S(2)}, u32[]{:S(2)}) collective-permute-start(bf16[2,34,1,256]{3,2,1,0:T(2,128)(2,1)S(1)} %get-tuple-element.36), channel_id=1, source_target_pairs={{0,1},{1,2},{2,3},{3,4},{4,5},{5,6},{6,7},{7,8},{8,9},{9,10},{10,1... | collective-permute-start | bytes 104456 | tf_op jit(solution)/shard_map/ppermute | solution.py:20
  34.9 3.1 %copy-start.2 = (bf16[2,34,49,256]{3,2,1,0:T(8,128)(2,1)}, bf16[2,34,49,256]{3,2,1,0:T(8,128)(2,1)S(1)}, u32[]{:S(2)}) copy-start(bf16[2,34,49,256]{3,2,1,0:T(8,128)(2,1)S(1)} %get-tuple-element.33) | copy-start | bytes 5117956
  41.5 1.9 copy-start.12
  41.5 1.9 copy-start.19
  43.4 2.2 copy-start.6
  43.4 2.2 copy-start.18
  45.6 1.7 copy-start.4
  48.0 91.1 %collective-permute-start.9 = (bf16[2,1,48,256]{3,2,1,0:T(8,128)(2,1)}, bf16[2,1,48,256]{3,2,1,0:T(8,128)(2,1)}, u32[]{:S(2)}, u32[]{:S(2)}) collective-permute-start(bf16[2,1,48,256]{3,2,1,0:T(8,128)(2,1)} %get-tuple-element.37), channel_id=1, source_target_pairs={{16,0},{32,16},{48,32},{64,48},{80,64},{96,80},{112,96},{17,1},{33... | collective-permute-start | bytes 147464 | tf_op jit(solution)/shard_map/ppermute | solution.py:21
  49.2 88.8 %collective-permute-start.6 = (bf16[2,1,48,256]{3,2,1,0:T(8,128)(2,1)}, bf16[2,1,48,256]{3,2,1,0:T(8,128)(2,1)}, u32[]{:S(2)}, u32[]{:S(2)}) collective-permute-start(bf16[2,1,48,256]{3,2,1,0:T(8,128)(2,1)} %get-tuple-element.37), channel_id=1, source_target_pairs={{0,8},{1,9},{2,10},{3,11},{4,12},{5,13},{6,14},{7,15},{8,0},{9,1},... | collective-permute-start | bytes 147464 | tf_op jit(solution)/shard_map/ppermute | solution.py:10
  52.1 87.0 %collective-permute-start.8 = (bf16[2,1,48,256]{3,2,1,0:T(8,128)(2,1)}, bf16[2,1,48,256]{3,2,1,0:T(8,128)(2,1)}, u32[]{:S(2)}, u32[]{:S(2)}) collective-permute-start(bf16[2,1,48,256]{3,2,1,0:T(8,128)(2,1)} %get-tuple-element.38), channel_id=1, source_target_pairs={{0,8},{1,9},{2,10},{3,11},{4,12},{5,13},{6,14},{7,15},{8,0},{9,1},... | collective-permute-start | bytes 147464 | tf_op jit(solution)/shard_map/ppermute | solution.py:10
  52.3 85.8 %collective-permute-start.7 = (bf16[2,1,48,256]{3,2,1,0:T(8,128)(2,1)}, bf16[2,1,48,256]{3,2,1,0:T(8,128)(2,1)}, u32[]{:S(2)}, u32[]{:S(2)}) collective-permute-start(bf16[2,1,48,256]{3,2,1,0:T(8,128)(2,1)} %get-tuple-element.38), channel_id=1, source_target_pairs={{0,16},{16,32},{32,48},{48,64},{64,80},{80,96},{96,112},{1,17},{17... | collective-permute-start | bytes 147464 | tf_op jit(solution)/shard_map/ppermute | solution.py:20
  64.2 2.8 copy-start.3
  68.4 1.4 copy-start.1
  72.6 1.3 copy-start.15
  76.6 0.7 copy-start.20
  76.6 3.8 %copy-start.22 = (f32[16]{0:T(128)S(1)}, f32[16]{0:T(128)}, u32[]{:S(2)}) copy-start(f32[16]{0:T(128)} %copy-done.21) | copy-start | bytes 196
  76.6 4.7 %copy-start.23 = (f32[256]{0:T(256)S(1)}, f32[256]{0:T(256)}, u32[]{:S(2)}) copy-start(f32[256]{0:T(256)} %get-tuple-element.43) | copy-start | bytes 3076
  76.6 62.3 %copy-start.9 = (bf16[9,256,256]{2,1,0:T(8,128)(2,1)S(1)}, bf16[9,256,256]{2,1,0:T(8,128)(2,1)}, u32[]{:S(2)}) copy-start(bf16[9,256,256]{2,1,0:T(8,128)(2,1)} %param.5) | copy-start | bytes 3538948
  76.7 224.9 %all-reduce.5.cloned.1.call-start = ((), (), s32[]{:S(2)}) async-start(), calls=%async_computation.1 | async-start | bytes 4718592 | tf_op jit(solution)/shard_map/psum | solution.py:129
  140.1 5.1 %collective-permute-start.11 = (bf16[2,34,1,256]{3,2,1,0:T(2,128)(2,1)S(1)}, bf16[2,34,1,256]{3,2,1,0:T(2,128)(2,1)S(1)}, u32[]{:S(2)}, u32[]{:S(2)}) collective-permute-start(bf16[2,34,1,256]{3,2,1,0:T(2,128)(2,1)S(1)} %get-tuple-element.31), channel_id=1, source_target_pairs={{1,0},{2,1},{3,2},{4,3},{5,4},{6,5},{7,6},{8,7},{9,8},{10,9},{11,1... | collective-permute-start | bytes 104456 | tf_op jit(solution)/shard_map/ppermute | solution.py:21
  140.9 4.3 %collective-permute-start.10 = (bf16[2,34,1,256]{3,2,1,0:T(2,128)(2,1)S(1)}, bf16[2,34,1,256]{3,2,1,0:T(2,128)(2,1)S(1)}, u32[]{:S(2)}, u32[]{:S(2)}) collective-permute-start(bf16[2,34,1,256]{3,2,1,0:T(2,128)(2,1)S(1)} %get-tuple-element.32), channel_id=1, source_target_pairs={{0,1},{1,2},{2,3},{3,4},{4,5},{5,6},{6,7},{7,8},{8,9},{9,10},{10,1... | collective-permute-start | bytes 104456 | tf_op jit(solution)/shard_map/ppermute | solution.py:20
  146.3 1.4 copy-start.7
  147.8 1.5 slice-start
  155.6 1.9 copy-start.5
  155.6 2.9 copy-start.13
  171.3 3.1 copy-start.11
  174.5 1.4 copy-start.10
Sparse Core Ops, SparseCore 0:
  76.7 94.5 all-reduce.2
  173.8 127.6 all-reduce.4
